TPU v7x, 32 devices: a whole 2x2x4 slice. The times are simulated.
32 devices in a mesh: dp: 8 (over y, x, core), tensor: 4 (over z).
Axes of the slice: x: 2, y: 2, z: 4, core: 2. Of those that a mesh axis runs over, the one named last changes fastest.
Arguments:
- inputs: bfloat16 [16384, 768], P(('dp', 'tensor')), may hold values from -6 to 6
- out_grad: bfloat16 [16384, 768], P(('dp', 'tensor')), may hold values from -6 to 6
- seq_lengths: int32 [8, 3], P('dp'), may hold values from 1 to 1024, 2048 in all within a row
- balance: int32 [8, 2048], P('dp'), may hold values from 0 to 2047, each once within a row
- clusters: int32 [8, 12, 2048], P('dp', 'tensor'), may hold values from 0 to 2047, each once within a row
- query_weight: bfloat16 [768, 768], P('dp', 'tensor'), may hold values from -0.21875 to 0.21875
- query_bias: float32 [768], P('tensor'), may hold values from -3 to 3
- key_weight: bfloat16 [768, 768], P('dp', 'tensor'), may hold values from -0.21875 to 0.21875
- value_weight: bfloat16 [768, 768], P('dp', 'tensor'), may hold values from -0.21875 to 0.21875
- value_bias: float32 [768], P('tensor'), may hold values from -3 to 3
- out_weight: bfloat16 [768, 768], P('tensor', 'dp'), may hold values from -0.875 to 0.875
- out_bias: float32 [768], replicated, may hold values from -3 to 3
- norm1_gain: float32 [768], replicated, may hold values from 0.1 to 1.9
- norm1_bias: float32 [768], replicated, may hold values from -3 to 3
- up_weight: bfloat16 [768, 3072], P('dp', 'tensor'), may hold values from -0.21875 to 0.21875
- up_bias: float32 [3072], P('tensor'), may hold values from -3 to 3
- down_weight: bfloat16 [3072, 768], P('tensor', 'dp'), may hold values from -0.109375 to 0.109375
- down_bias: float32 [768], replicated, may hold values from -3 to 3
- norm2_gain: float32 [768], replicated, may hold values from 0.1 to 1.9
- norm2_bias: float32 [768], replicated, may hold values from -3 to 3
Outputs:
- layer_out: bfloat16 [16384, 768], P(('dp', 'tensor'))
- grad_inputs: float32 [16384, 768], P(('dp', 'tensor'))
- grad_query_weight: float32 [768, 768], P('dp', 'tensor')
- grad_query_bias: float32 [768], P('tensor')
- grad_key_weight: float32 [768, 768], P('dp', 'tensor')
- grad_value_weight: float32 [768, 768], P('dp', 'tensor')
- grad_value_bias: float32 [768], P('tensor')
- grad_out_weight: float32 [768, 768], P('tensor', 'dp')
- grad_out_bias: float32 [768], replicated
- grad_norm1_gain: float32 [768], replicated
- grad_norm1_bias: float32 [768], replicated
- grad_up_weight: float32 [768, 3072], P('dp', 'tensor')
- grad_up_bias: float32 [3072], P('tensor')
- grad_down_weight: float32 [3072, 768], P('tensor', 'dp')
- grad_down_bias: float32 [768], replicated
- grad_norm2_gain: float32 [768], replicated
- grad_norm2_bias: float32 [768], replicated
Inputs may be any that keep to these rules, and one draw needn't show every extreme that they name: `seq_lengths`: each group's lengths sum to 2048; the largest in each group is exactly 1024. `balance`: each group's row is a permutation of its 2048 token indices. `clusters`: each head's row of a group is a permutation of the 2048 balanced positions.
All inputs are finite; a program needn't handle non-finite values.
Results may differ from a plain program's by a relative error of at most 0.019.
Values may be sent and summed in bfloat16 or wider, within the bound.
No kernel may reach another device: no remote copies, remote signals or barrier semaphores. Data moves between devices by JAX's collectives and lax.ppermute only.
A program may use at most 128 MiB of HBM per device.

v0:
```python
import jax
import jax.numpy as jnp
from jax import lax
from jax.sharding import PartitionSpec as P

HD = 64
CL = 128


def layer_norm(values_in, gain, shift):
    center = values_in - jnp.mean(values_in, axis=-1, keepdims=True)
    variance = jnp.mean(center * center, axis=-1, keepdims=True)
    return center * lax.rsqrt(variance + 1e-06) * gain + shift


def gelu_tanh(values_in):
    return jax.nn.gelu(values_in, approximate=True)


def product(left, right):
    return jnp.dot(left, right, preferred_element_type=jnp.float32)


def product_nt(left, right):
    return lax.dot_general(
        left, right, (((1,), (1,)), ((), ())), preferred_element_type=jnp.float32
    )


def product_tn(left, right):
    return lax.dot_general(
        left, right, (((0,), (0,)), ((), ())), preferred_element_type=jnp.float32
    )


def to_slots(values_in, slot_order):
    token_count = values_in.shape[0]
    head_count = slot_order.shape[0]
    per_head = values_in.reshape(token_count, head_count, HD).transpose(1, 0, 2)
    picked = jnp.take_along_axis(per_head, slot_order[:, :, None], axis=1)
    return picked.reshape(head_count, token_count // CL, CL, HD)


def to_tokens(slots, token_place):
    head_count = slots.shape[0]
    flat_slots = slots.reshape(head_count, -1, HD)
    placed = jnp.take_along_axis(flat_slots, token_place[:, :, None], axis=1)
    return placed.transpose(1, 0, 2).reshape(flat_slots.shape[1], head_count * HD)


def masked_scores(query_slots, key_slots, segment_slots):
    raw_scores = jnp.einsum(
        "hcqd,hckd->hcqk", query_slots, key_slots, preferred_element_type=jnp.float32
    ) * HD ** (-0.5)
    same_doc = segment_slots[:, :, :, None] == segment_slots[:, :, None, :]
    return jnp.where(same_doc, raw_scores, -1e30)


def local(
    inputs,
    out_grad,
    seq_lengths,
    balance,
    clusters,
    query_weight,
    query_bias,
    key_weight,
    value_weight,
    value_bias,
    out_weight,
    out_bias,
    norm1_gain,
    norm1_bias,
    up_weight,
    up_bias,
    down_weight,
    down_bias,
    norm2_gain,
    norm2_bias,
):
    row_count = inputs.shape[0]
    tensor_size = lax.axis_size("tensor")
    tensor_rank = lax.axis_index("tensor")
    group_rows = row_count * tensor_size
    local_width = query_weight.shape[1]
    local_hidden = up_weight.shape[1]
    query_full, key_full, value_full, out_full, up_rows, down_cols = (
        lax.all_gather(query_weight, "dp", axis=0, tiled=True),
        lax.all_gather(key_weight, "dp", axis=0, tiled=True),
        lax.all_gather(value_weight, "dp", axis=0, tiled=True),
        lax.all_gather(out_weight, "dp", axis=1, tiled=True),
        lax.all_gather(up_weight, "dp", axis=0, tiled=True),
        lax.all_gather(down_weight, "dp", axis=1, tiled=True),
    )
    positions = jnp.arange(group_rows, dtype=jnp.int32)
    bounds = jnp.cumsum(seq_lengths[0])
    segment = jnp.sum((positions[:, None] >= bounds[None, :]).astype(jnp.int32), axis=1)
    slot_order = jnp.take(balance[0], clusters[0], axis=0)
    token_place = jax.vmap(
        lambda row_order: jnp.zeros((group_rows,), jnp.int32).at[row_order].set(positions)
    )(slot_order)
    segment_slots = jnp.take(segment, slot_order, axis=0).reshape(
        slot_order.shape[0], group_rows // CL, CL
    )
    inputs_all = lax.all_gather(inputs, "tensor", axis=0, tiled=True)
    query_rows = (product(inputs_all, query_full) + query_bias).astype(jnp.bfloat16)
    key_rows = product(inputs_all, key_full).astype(jnp.bfloat16)
    value_rows = (product(inputs_all, value_full) + value_bias).astype(jnp.bfloat16)
    query_slots = to_slots(query_rows, slot_order)
    key_slots = to_slots(key_rows, slot_order)
    value_slots = to_slots(value_rows, slot_order)
    scores = masked_scores(query_slots, key_slots, segment_slots)
    top_score = jnp.max(scores, axis=-1, keepdims=True)
    log_total = top_score + jnp.log(jnp.sum(jnp.exp(scores - top_score), axis=-1, keepdims=True))
    prob_low = jnp.exp(scores - log_total).astype(jnp.bfloat16)
    context_slots = jnp.einsum(
        "hcqk,hckd->hcqd", prob_low, value_slots, preferred_element_type=jnp.float32
    ).astype(jnp.bfloat16)
    context = to_tokens(context_slots, token_place)
    attention = lax.psum_scatter(
        product(context, out_full).astype(jnp.bfloat16), "tensor", scatter_dimension=0, tiled=True
    ).astype(jnp.float32)
    summed = inputs.astype(jnp.float32) + attention + out_bias
    normed = layer_norm(summed, norm1_gain, norm1_bias)
    normed_low = normed.astype(jnp.bfloat16)
    normed_all = lax.all_gather(normed_low, "tensor", axis=0, tiled=True)
    up_value = product(normed_all, up_rows) + up_bias
    active = gelu_tanh(up_value).astype(jnp.bfloat16)
    feed = lax.psum_scatter(
        product(active, down_cols).astype(jnp.bfloat16), "tensor", scatter_dimension=0, tiled=True
    ).astype(jnp.float32)
    pre_norm = normed + feed + down_bias
    layer_out = layer_norm(pre_norm, norm2_gain, norm2_bias).astype(jnp.bfloat16)
    _, norm2_pull = jax.vjp(layer_norm, pre_norm, norm2_gain, norm2_bias)
    grad_pre, grad_gain_two, grad_shift_two = norm2_pull(out_grad.astype(jnp.float32))
    grad_pre_low = grad_pre.astype(jnp.bfloat16)
    _, gelu_pull = jax.vjp(gelu_tanh, up_value)
    grad_pre_all = lax.all_gather(grad_pre_low, "tensor", axis=0, tiled=True)
    grad_up = gelu_pull(product_nt(grad_pre_all, down_cols))[0].astype(jnp.bfloat16)
    grad_down_local = product_tn(active, grad_pre_all)
    grad_up_local = product_tn(normed_all, grad_up)
    grad_normed_part = lax.psum_scatter(
        product_nt(grad_up, up_rows).astype(jnp.bfloat16), "tensor", scatter_dimension=0, tiled=True
    ).astype(jnp.float32)
    grad_up_bias_full = lax.dynamic_update_slice(
        jnp.zeros((local_hidden * tensor_size,), jnp.float32),
        jnp.sum(grad_up.astype(jnp.float32), axis=0),
        (tensor_rank * local_hidden,),
    )
    grad_normed = grad_pre + grad_normed_part
    _, norm1_pull = jax.vjp(layer_norm, summed, norm1_gain, norm1_bias)
    grad_summed, grad_gain_one, grad_shift_one = norm1_pull(grad_normed)
    grad_summed_low = grad_summed.astype(jnp.bfloat16)
    grad_summed_all = lax.all_gather(grad_summed_low, "tensor", axis=0, tiled=True)
    grad_out_local = product_tn(context, grad_summed_all)
    grad_context = product_nt(grad_summed_all, out_full).astype(jnp.bfloat16)
    grad_context_slots = to_slots(grad_context, slot_order)
    again_scores = masked_scores(query_slots, key_slots, segment_slots)
    prob_values = jnp.exp(again_scores - log_total)
    again_low = prob_values.astype(jnp.bfloat16)
    grad_prob = jnp.einsum(
        "hcqd,hckd->hcqk", grad_context_slots, value_slots, preferred_element_type=jnp.float32
    )
    grad_scores = (
        prob_values * (grad_prob - jnp.sum(prob_values * grad_prob, axis=-1, keepdims=True))
    ).astype(jnp.bfloat16)
    grad_query_slots = (
        jnp.einsum("hcqk,hckd->hcqd", grad_scores, key_slots, preferred_element_type=jnp.float32)
        * HD ** (-0.5)
    ).astype(jnp.bfloat16)
    grad_key_slots = (
        jnp.einsum("hcqk,hcqd->hckd", grad_scores, query_slots, preferred_element_type=jnp.float32)
        * HD ** (-0.5)
    ).astype(jnp.bfloat16)
    grad_value_slots = jnp.einsum(
        "hcqk,hcqd->hckd", again_low, grad_context_slots, preferred_element_type=jnp.float32
    ).astype(jnp.bfloat16)
    grad_query = to_tokens(grad_query_slots, token_place)
    grad_key = to_tokens(grad_key_slots, token_place)
    grad_value = to_tokens(grad_value_slots, token_place)
    grad_query_local = product_tn(inputs_all, grad_query)
    grad_key_local = product_tn(inputs_all, grad_key)
    grad_value_local = product_tn(inputs_all, grad_value)
    grad_inputs = grad_summed + lax.psum_scatter(
        (
            product_nt(grad_query, query_full)
            + product_nt(grad_key, key_full)
            + product_nt(grad_value, value_full)
        ).astype(jnp.bfloat16),
        "tensor",
        scatter_dimension=0,
        tiled=True,
    ).astype(jnp.float32)
    width_full = local_width * tensor_size

    def spread_width(part_sum):
        return lax.dynamic_update_slice(
            jnp.zeros((width_full,), jnp.float32), part_sum, (tensor_rank * local_width,)
        )

    (
        query_bias_sum,
        value_bias_sum,
        up_bias_sum,
        grad_out_bias,
        grad_norm1_gain,
        grad_norm1_bias,
        grad_down_bias,
        grad_norm2_gain,
        grad_norm2_bias,
    ) = lax.psum(
        (
            spread_width(jnp.sum(grad_query.astype(jnp.float32), axis=0)),
            spread_width(jnp.sum(grad_value.astype(jnp.float32), axis=0)),
            grad_up_bias_full,
            jnp.sum(grad_summed, axis=0),
            grad_gain_one,
            grad_shift_one,
            jnp.sum(grad_pre, axis=0),
            grad_gain_two,
            grad_shift_two,
        ),
        ("dp", "tensor"),
    )
    grad_query_bias = lax.dynamic_slice_in_dim(
        query_bias_sum, tensor_rank * local_width, local_width, 0
    )
    grad_value_bias = lax.dynamic_slice_in_dim(
        value_bias_sum, tensor_rank * local_width, local_width, 0
    )
    grad_up_bias = lax.dynamic_slice_in_dim(
        up_bias_sum, tensor_rank * local_hidden, local_hidden, 0
    )
    (
        grad_query_weight,
        grad_key_weight,
        grad_value_weight,
        grad_out_weight,
        grad_up_weight,
        grad_down_weight,
    ) = (
        lax.psum_scatter(grad_query_local, "dp", scatter_dimension=0, tiled=True),
        lax.psum_scatter(grad_key_local, "dp", scatter_dimension=0, tiled=True),
        lax.psum_scatter(grad_value_local, "dp", scatter_dimension=0, tiled=True),
        lax.psum_scatter(grad_out_local, "dp", scatter_dimension=1, tiled=True),
        lax.psum_scatter(grad_up_local, "dp", scatter_dimension=0, tiled=True),
        lax.psum_scatter(grad_down_local, "dp", scatter_dimension=1, tiled=True),
    )
    return (
        layer_out,
        grad_inputs,
        grad_query_weight,
        grad_query_bias,
        grad_key_weight,
        grad_value_weight,
        grad_value_bias,
        grad_out_weight,
        grad_out_bias,
        grad_norm1_gain,
        grad_norm1_bias,
        grad_up_weight,
        grad_up_bias,
        grad_down_weight,
        grad_down_bias,
        grad_norm2_gain,
        grad_norm2_bias,
    )


def solution(mesh):
    in_specs = (
        P(("dp", "tensor"), None),
        P(("dp", "tensor"), None),
        P("dp", None),
        P("dp", None),
        P("dp", "tensor", None),
        P("dp", "tensor"),
        P("tensor"),
        P("dp", "tensor"),
        P("dp", "tensor"),
        P("tensor"),
        P("tensor", "dp"),
        P(),
        P(),
        P(),
        P("dp", "tensor"),
        P("tensor"),
        P("tensor", "dp"),
        P(),
        P(),
        P(),
    )
    out_specs = (
        P(("dp", "tensor"), None),
        P(("dp", "tensor"), None),
        P("dp", "tensor"),
        P("tensor"),
        P("dp", "tensor"),
        P("dp", "tensor"),
        P("tensor"),
        P("tensor", "dp"),
        P(),
        P(),
        P(),
        P("dp", "tensor"),
        P("tensor"),
        P("tensor", "dp"),
        P(),
        P(),
        P(),
    )
    return jax.shard_map(local, mesh=mesh, in_specs=in_specs, out_specs=out_specs, check_vma=False)
```

profile of v0, /device:TPU:0, one launch (start us, length us, event | category | flops | bytes accessed | tf_op | source)
XLA Modules:
  0.0 1201.1 jit_solution(17774574574458499164)
XLA Ops:
  9.7 34.3 %gather_fusion = s32[6144]{0:T(1024)S(1)} fusion(s32[2048]{0:T(1024)S(1)} %bitcast.160, s32[6144]{0:T(1024)S(1)} %broadcast_clamp_fusion.1), kind=kCustom, calls=%fused_computation.clone | custom fusion | bytes 73728 | tf_op jit(solution)/shard_map/jit(_take)/gather | solution.py:98
  44.6 23.0 %scatter_custom_fusion = s32[6144]{0:T(1024)S(1)} fusion(s32[6144]{0:T(1024)S(1)} %reshape.282, s32[6144]{0:T(1024)S(1)} %reshape.284, s32[]{:T(128)} %constant.20.clone.1), kind=kCustom, calls=%fused_computation.120 | custom fusion | bytes 24580
  67.9 34.3 %gather_fusion.1 = s32[6144]{0:T(1024)S(1)} fusion(s32[2048]{0:T(1024)S(1)} %convert_reduce_fusion.4, s32[6144]{0:T(1024)S(1)} %broadcast_clamp_fusion), kind=kCustom, calls=%fused_computation.2.clone | custom fusion | bytes 73728 | tf_op jit(solution)/shard_map/jit(_take)/gather | solution.py:102
  148.3 32.3 %gather_fusion.4 = bf16[6144,64]{1,0:T(8,128)(2,1)S(1)} fusion(bf16[3,2048,64]{2,1,0:T(8,128)(2,1)S(1)} %bitcast.163, s32[6144]{0:T(1024)S(1)} %reshape.300), kind=kCustom, calls=%fused_computation.4.clone | custom fusion | bytes 1622016 | tf_op jit(solution)/shard_map/jit(take_along_axis)/gather | solution.py:40
  186.0 32.3 %gather_fusion.3 = bf16[6144,64]{1,0:T(8,128)(2,1)S(1)} fusion(bf16[3,2048,64]{2,1,0:T(8,128)(2,1)S(1)} %bitcast.164, s32[6144]{0:T(1024)S(1)} %reshape.300), kind=kCustom, calls=%fused_computation.3.clone | custom fusion | bytes 1622016 | tf_op jit(solution)/shard_map/jit(take_along_axis)/gather | solution.py:40
  223.7 32.3 %gather_fusion.2 = bf16[6144,64]{1,0:T(8,128)(2,1)S(1)} fusion(bf16[3,2048,64]{2,1,0:T(8,128)(2,1)S(1)} %bitcast.165, s32[6144]{0:T(1024)S(1)} %reshape.300), kind=kCustom, calls=%fused_computation.1.clone | custom fusion | bytes 1622016 | tf_op jit(solution)/shard_map/jit(take_along_axis)/gather | solution.py:40
  264.6 32.3 %gather_fusion.5 = bf16[6144,64]{1,0:T(8,128)(2,1)S(1)} fusion(bf16[3,2048,64]{2,1,0:T(8,128)(2,1)S(1)} %bitcast.166, s32[6144]{0:T(1024)S(1)} %reshape.312), kind=kCustom, calls=%fused_computation.5.clone | custom fusion | bytes 1622016 | tf_op jit(solution)/shard_map/jit(take_along_axis)/gather | solution.py:47
  302.2 59.9 %reduce-scatter.19.cloned.1.call-done = bf16[512,768]{1,0:T(8,128)(2,1)} async-done(((bf16[2048,768]{1,0:T(8,128)(2,1)}), bf16[512,768]{1,0:T(8,128)(2,1)}) %reduce-scatter.19.cloned.1.call-update) | async-done | bytes 786448 | tf_op jit(solution)/shard_map/reduce_scatter | solution.py:120
  367.3 62.8 %all-gather.9.cloned.1.call-done = bf16[2048,768]{1,0:T(8,128)(2,1)} async-done(((bf16[512,768]{1,0:T(8,128)(2,1)}), bf16[2048,768]{1,0:T(8,128)(2,1)}) %all-gather.9.cloned.1.call-update) | async-done | bytes 3145744 | tf_op jit(solution)/shard_map/all_gather | solution.py:126
  439.8 14.6 %all-gather.13.cloned.1.call-done = bf16[768,768]{0,1:T(8,128)(2,1)} async-done(((bf16[768,96]{0,1:T(8,128)(2,1)}), bf16[768,768]{0,1:T(8,128)(2,1)}) %all-gather.13.cloned.1.call-update) | async-done | bytes 1179664 | tf_op jit(solution)/shard_map/all_gather | solution.py:93
  461.0 60.3 %reduce-scatter.21.cloned.1.call-done = bf16[512,768]{1,0:T(8,128)(2,1)} async-done(((bf16[2048,768]{1,0:T(8,128)(2,1)}), bf16[512,768]{1,0:T(8,128)(2,1)}) %reduce-scatter.21.cloned.1.call-update) | async-done | bytes 786448 | tf_op jit(solution)/shard_map/reduce_scatter | solution.py:129
  528.3 63.3 %all-gather.15.cloned.1.call-done = bf16[2048,768]{1,0:T(8,128)(2,1)} async-done(((bf16[512,768]{1,0:T(8,128)(2,1)}), bf16[2048,768]{1,0:T(8,128)(2,1)}) %all-gather.15.cloned.1.call-update) | async-done | bytes 3145744 | tf_op jit(solution)/shard_map/all_gather | solution.py:138
  606.2 59.0 %reduce-scatter.23.cloned.1.call-done = bf16[512,768]{1,0:T(8,128)(2,1)} async-done(((bf16[2048,768]{1,0:T(8,128)(2,1)}), bf16[512,768]{1,0:T(8,128)(2,1)}) %reduce-scatter.23.cloned.1.call-update) | async-done | bytes 786448 | tf_op jit(solution)/shard_map/reduce_scatter | solution.py:142
  671.2 63.1 %all-gather.17.cloned.1.call-done = bf16[2048,768]{1,0:T(8,128)(2,1)} async-done(((bf16[512,768]{1,0:T(8,128)(2,1)}), bf16[2048,768]{1,0:T(8,128)(2,1)}) %all-gather.17.cloned.1.call-update) | async-done | bytes 3145744 | tf_op jit(solution)/shard_map/all_gather | solution.py:154
  738.2 60.6 %gather_fusion.6 = bf16[6144,64]{1,0:T(8,128)(2,1)} fusion(bf16[3,2048,64]{2,1,0:T(8,128)(2,1)S(1)} %bitcast.161, s32[6144]{0:T(1024)S(1)} %reshape.300), kind=kCustom, calls=%fused_computation.6.clone | custom fusion | bytes 1622016 | tf_op jit(solution)/shard_map/jit(take_along_axis)/gather | solution.py:40
  814.8 32.3 %gather_fusion.9 = bf16[6144,64]{1,0:T(8,128)(2,1)S(1)} fusion(bf16[3,2048,64]{2,1,0:T(8,128)(2,1)S(1)} %bitcast.167, s32[6144]{0:T(1024)S(1)} %reshape.312), kind=kCustom, calls=%fused_computation.9.clone | custom fusion | bytes 1622016 | tf_op jit(solution)/shard_map/jit(take_along_axis)/gather | solution.py:47
  850.3 32.3 %gather_fusion.7 = bf16[6144,64]{1,0:T(8,128)(2,1)S(1)} fusion(bf16[3,2048,64]{2,1,0:T(8,128)(2,1)S(1)} %bitcast.168, s32[6144]{0:T(1024)S(1)} %reshape.312), kind=kCustom, calls=%fused_computation.7.clone | custom fusion | bytes 1622016 | tf_op jit(solution)/shard_map/jit(take_along_axis)/gather | solution.py:47
  885.8 32.3 %gather_fusion.8 = bf16[6144,64]{1,0:T(8,128)(2,1)S(1)} fusion(bf16[3,2048,64]{2,1,0:T(8,128)(2,1)S(1)} %bitcast.162, s32[6144]{0:T(1024)S(1)} %reshape.312), kind=kCustom, calls=%fused_computation.8.clone | custom fusion | bytes 1622016 | tf_op jit(solution)/shard_map/jit(take_along_axis)/gather | solution.py:47
  957.0 43.1 %all-reduce = (f32[768]{0:T(1024)S(1)}, f32[768]{0:T(1024)S(1)}, f32[768]{0:T(1024)}, f32[768]{0:T(1024)}, f32[768]{0:T(1024)}, /*index=5*/f32[3072]{0:T(1024)S(1)}, f32[768]{0:T(1024)}, f32[768]{0:T(1024)}, f32[768]{0:T(1024)}) all-reduce(f32[768]{0:T(1024)S(1)} %dynamic_update_slice.9, ...), channel_id=1, replica_groups=mesh['dp'=8,'tensor'=4] {'dp','tensor'}, use_global_device_ids=true, to_apply=%region_20.23 | all-reduce | flops 9216 | bytes 73728 | tf_op jit(solution)/shard_map/psum | solution.py:211
  1006.2 25.1 %reduce-scatter.27.cloned.1.call-done = f32[96,768]{1,0:T(8,128)} async-done(((f32[768,768]{1,0:T(8,128)}), f32[96,768]{1,0:T(8,128)}) %reduce-scatter.27.cloned.1.call-update) | async-done | bytes 294928 | tf_op jit(solution)/shard_map/reduce_scatter | solution.py:246
  1031.3 46.5 %reduce-scatter.29.cloned.1.call-done = f32[768,96]{0,1:T(8,128)} async-done(((f32[768,768]{0,1:T(8,128)}), f32[768,96]{0,1:T(8,128)}) %reduce-scatter.29.cloned.1.call-update) | async-done | bytes 294928 | tf_op jit(solution)/shard_map/reduce_scatter | solution.py:247
  1077.8 38.7 %reduce-scatter.35.cloned.1.call-done = f32[96,192]{1,0:T(8,128)} async-done(((f32[768,192]{1,0:T(8,128)}), f32[96,192]{1,0:T(8,128)}) %reduce-scatter.35.cloned.1.call-update) | async-done | bytes 73744
  1116.5 38.5 %reduce-scatter.31.cloned.1.call-done = f32[96,192]{1,0:T(8,128)} async-done(((f32[768,192]{1,0:T(8,128)}), f32[96,192]{1,0:T(8,128)}) %reduce-scatter.31.cloned.1.call-update) | async-done | bytes 73744
  1155.0 38.7 %reduce-scatter.33.cloned.1.call-done = f32[96,192]{1,0:T(8,128)} async-done(((f32[768,192]{1,0:T(8,128)}), f32[96,192]{1,0:T(8,128)}) %reduce-scatter.33.cloned.1.call-update) | async-done | bytes 73744
  (256 shorter events, 192.9 us)
Async XLA Ops:
  8.0 136.3 %all-gather.7.cloned.1.call-start = ((), (), s32[]{:S(2)}) async-start(), calls=%async_computation.10 | async-start | bytes 3932160 | tf_op jit(solution)/shard_map/all_gather | solution.py:105
  8.8 353.3 %reduce-scatter.19.cloned.1.call-start = ((), (), s32[]{:S(2)}) async-start(), calls=%async_computation.11 | async-start | bytes 3932160 | tf_op jit(solution)/shard_map/reduce_scatter | solution.py:120
  67.9 66.7 %copy-start.38 = (bf16[96,192]{1,0:T(8,128)(2,1)S(1)}, bf16[96,192]{1,0:T(8,128)(2,1)}, u32[]{:S(2)}) copy-start(bf16[96,192]{1,0:T(8,128)(2,1)} %param.32) | copy-start | bytes 110596
  67.9 76.4 %copy-start.49 = (f32[192]{0:T(256)S(1)}, f32[192]{0:T(256)}, u32[]{:S(2)}) copy-start(f32[192]{0:T(256)} %param.33) | copy-start | bytes 2308
  298.6 63.5 %copy-start.33 = (f32[768]{0:T(1024)S(1)}, f32[768]{0:T(1024)}, u32[]{:S(2)}) copy-start(f32[768]{0:T(1024)} %param.35) | copy-start | bytes 9220
  301.3 63.9 %copy-start.35 = (f32[768]{0:T(1024)S(1)}, f32[768]{0:T(1024)}, u32[]{:S(2)}) copy-start(f32[768]{0:T(1024)} %param.36) | copy-start | bytes 9220
  301.3 63.9 %copy-start.41 = (f32[768]{0:T(1024)S(1)}, f32[768]{0:T(1024)}, u32[]{:S(2)}) copy-start(f32[768]{0:T(1024)} %param.37) | copy-start | bytes 9220
  301.3 65.9 %all-gather.11.cloned.1.call-start = ((), (), s32[]{:S(2)}) async-start(), calls=%async_computation.13 | async-start | bytes 1327104 | tf_op jit(solution)/shard_map/all_gather | solution.py:92
  301.9 128.1 %copy-start.48 = (f32[768]{0:T(1024)S(1)}, f32[768]{0:T(1024)}, u32[]{:S(2)}) copy-start(f32[768]{0:T(1024)} %param.39) | copy-start | bytes 9220
  301.9 128.1 %all-gather.9.cloned.1.call-start = ((), (), s32[]{:S(2)}) async-start(), calls=%async_computation.12 | async-start | bytes 3932160 | tf_op jit(solution)/shard_map/all_gather | solution.py:126
  366.6 87.8 %all-gather.13.cloned.1.call-start = ((), (), s32[]{:S(2)}) async-start(), calls=%async_computation.14 | async-start | bytes 1327104 | tf_op jit(solution)/shard_map/all_gather | solution.py:93
  367.2 154.1 %reduce-scatter.21.cloned.1.call-start = ((), (), s32[]{:S(2)}) async-start(), calls=%async_computation.15 | async-start | bytes 3932160 | tf_op jit(solution)/shard_map/reduce_scatter | solution.py:129
  461.0 130.6 %all-gather.15.cloned.1.call-start = ((), (), s32[]{:S(2)}) async-start(), calls=%async_computation.16 | async-start | bytes 3932160 | tf_op jit(solution)/shard_map/all_gather | solution.py:138
  528.0 137.1 %reduce-scatter.23.cloned.1.call-start = ((), (), s32[]{:S(2)}) async-start(), calls=%async_computation.17 | async-start | bytes 3932160 | tf_op jit(solution)/shard_map/reduce_scatter | solution.py:142
  606.1 128.2 %all-gather.17.cloned.1.call-start = ((), (), s32[]{:S(2)}) async-start(), calls=%async_computation.18 | async-start | bytes 3932160 | tf_op jit(solution)/shard_map/all_gather | solution.py:154
  668.4 65.9 %copy-start.17 = (bf16[192,768]{0,1:T(8,128)(2,1)S(1)}, bf16[192,768]{0,1:T(8,128)(2,1)}, u32[]{:S(2)}) copy-start(bf16[192,768]{0,1:T(8,128)(2,1)} %all_gather.34) | copy-start | bytes 884740
  670.7 331.3 %reduce-scatter.37.cloned.1.call-start = ((), (), s32[]{:S(2)}) async-start(), calls=%async_computation.25 | async-start | bytes 884736
  813.7 189.9 %reduce-scatter.25.cloned.1.call-start = ((), (), s32[]{:S(2)}) async-start(), calls=%async_computation.19 | async-start | bytes 3932160 | tf_op jit(solution)/shard_map/reduce_scatter | solution.py:184
  925.5 105.8 %reduce-scatter.27.cloned.1.call-start = ((), (), s32[]{:S(2)}) async-start(), calls=%async_computation.20 | async-start | bytes 2654208 | tf_op jit(solution)/shard_map/reduce_scatter | solution.py:246
  933.4 144.4 %reduce-scatter.29.cloned.1.call-start = ((), (), s32[]{:S(2)}) async-start(), calls=%async_computation.21 | async-start | bytes 2654208 | tf_op jit(solution)/shard_map/reduce_scatter | solution.py:247
  940.7 175.7 %reduce-scatter.35.cloned.1.call-start = ((), (), s32[]{:S(2)}) async-start(), calls=%async_computation.24 | async-start | bytes 884736
  945.8 209.2 %reduce-scatter.31.cloned.1.call-start = ((), (), s32[]{:S(2)}) async-start(), calls=%async_computation.22 | async-start | bytes 884736
  950.9 242.8 %reduce-scatter.33.cloned.1.call-start = ((), (), s32[]{:S(2)}) async-start(), calls=%async_computation.23 | async-start | bytes 884736
  951.0 242.8 %copy-start.1 = (s32[1,2048]{1,0:T(1,128)S(1)}, s32[1,2048]{1,0:T(1,128)}, u32[]{:S(2)}) copy-start(s32[1,2048]{1,0:T(1,128)} %param.27) | copy-start | bytes 24580
  (45 other events, 759.4 us)
Sparse Core Ops, SparseCore 0:
  10.4 66.1 all-gather.6
  301.5 60.5 reduce-scatter.18
  528.2 63.4 all-gather.14
  670.9 63.4 all-gather.16
Sparse Core Ops, SparseCore 1:
  303.7 24.1 all-gather.10
  366.7 63.3 all-gather.8
  431.8 22.5 all-gather.12
  461.0 60.2 reduce-scatter.20
  606.2 58.9 reduce-scatter.22
  813.8 33.5 reduce-scatter.36
  925.5 59.6 reduce-scatter.24
  988.9 42.3 reduce-scatter.26
  1035.4 42.3 reduce-scatter.28
  1081.5 34.9 reduce-scatter.34
  1120.1 34.9 reduce-scatter.30
  1158.8 34.9 reduce-scatter.32
where the time goes:
time: 1210 us; the launch traced here: 1200 us
  waiting for transfers between devices  572 us (47%)
  local copies, waits for them, and re-layouts  417 us (34%)
  matrix products  85.4 us (7%)
  blocking collectives  84.9 us (7%)
  other arithmetic  23.4 us (2%)
  between operations  16.6 us (1%)
    gather x9, local copies, waits for them, and re-layouts, to_slots(): picked = jnp.take_along_axis(per_head, slot_order[:, :, None], axis=1)  164 us
    gather x9, local copies, waits for them, and re-layouts, to_tokens(): placed = jnp.take_along_axis(flat_slots, token_place[:, :, None], axis=1)  133 us
    unnamed x20, waiting for transfers between devices  118 us
    all_gather x1, waiting for transfers between devices, local(): grad_pre_all = lax.all_gather(grad_pre_low, 'tensor', axis=0, tiled=True)  63.3 us
    all_gather x1, waiting for transfers between devices, local(): lax.all_gather(grad_summed_low, 'tensor', axis=0, tiled=True)  63.1 us
    all_gather x1, waiting for transfers between devices, local(): normed_all = lax.all_gather(normed_low, 'tensor', axis=0, tiled=True)  62.8 us
    reduce_scatter x1, waiting for transfers between devices, local(): lax.psum_scatter(product(active, down_cols).astype(jnp.bfloat16), 'tensor...  60.3 us
    reduce_scatter x1, waiting for transfers between devices, local(): lax.psum_scatter(product(context, out_full).astype(jnp.bfloat16), 'tensor...  59.9 us
  transfers between devices with their start and end apart: 16, of which 12 were waited for; matrix products, arithmetic and copies ran while one was open for 21% of the time, Pallas kernels for 0%

commit v1 on v0

--- a/solution.py
+++ b/solution.py
@@ -209,18 +209,21 @@
         grad_norm2_gain,
         grad_norm2_bias,
     ) = lax.psum(
-        (
-            spread_width(jnp.sum(grad_query.astype(jnp.float32), axis=0)),
-            spread_width(jnp.sum(grad_value.astype(jnp.float32), axis=0)),
-            grad_up_bias_full,
-            jnp.sum(grad_summed, axis=0),
-            grad_gain_one,
-            grad_shift_one,
-            jnp.sum(grad_pre, axis=0),
-            grad_gain_two,
-            grad_shift_two,
+        lax.psum(
+            (
+                spread_width(jnp.sum(grad_query.astype(jnp.float32), axis=0)),
+                spread_width(jnp.sum(grad_value.astype(jnp.float32), axis=0)),
+                grad_up_bias_full,
+                jnp.sum(grad_summed, axis=0),
+                grad_gain_one,
+                grad_shift_one,
+                jnp.sum(grad_pre, axis=0),
+                grad_gain_two,
+                grad_shift_two,
+            ),
+            "tensor",
         ),
-        ("dp", "tensor"),
+        "dp",
     )
     grad_query_bias = lax.dynamic_slice_in_dim(
         query_bias_sum, tensor_rank * local_width, local_width, 0

time: 1210 us -> 1210 us (level)
    psum x1, blocking collectives: 43.1 us -> 19.2 us  [local(): lax.psum((spread_width(jnp.sum(grad_query.astype(jnp.float32), axis=0)),...]
    psum x0 -> x1, blocking collectives: none -> 23.7 us  [local(): lax.psum(lax.psum((spread_width(jnp.sum(grad_query.astype(jnp.float32), a...]
where the time goes in v1:
time: 1210 us; the launch traced here: 1200 us
  waiting for transfers between devices  573 us (47%)
  local copies, waits for them, and re-layouts  417 us (34%)
  matrix products  85.3 us (7%)
  blocking collectives  84.7 us (7%)
  other arithmetic  23.4 us (2%)
  between operations  16.6 us (1%)
    gather x9, local copies, waits for them, and re-layouts, to_slots(): picked = jnp.take_along_axis(per_head, slot_order[:, :, None], axis=1)  164 us
    gather x9, local copies, waits for them, and re-layouts, to_tokens(): placed = jnp.take_along_axis(flat_slots, token_place[:, :, None], axis=1)  133 us
    unnamed x20, waiting for transfers between devices  118 us
    all_gather x1, waiting for transfers between devices, local(): grad_pre_all = lax.all_gather(grad_pre_low, 'tensor', axis=0, tiled=True)  63.3 us
    all_gather x1, waiting for transfers between devices, local(): lax.all_gather(grad_summed_low, 'tensor', axis=0, tiled=True)  63.1 us
    all_gather x1, waiting for transfers between devices, local(): normed_all = lax.all_gather(normed_low, 'tensor', axis=0, tiled=True)  62.8 us
    reduce_scatter x1, waiting for transfers between devices, local(): lax.psum_scatter(product(active, down_cols).astype(jnp.bfloat16), 'tensor...  60.3 us
    reduce_scatter x1, waiting for transfers between devices, local(): lax.psum_scatter(product(context, out_full).astype(jnp.bfloat16), 'tensor...  59.9 us
  transfers between devices with their start and end apart: 16, of which 12 were waited for; matrix products, arithmetic and copies ran while one was open for 21% of the time, Pallas kernels for 0%

profile of v1, /device:TPU:0, one launch (start us, length us, event | category | flops | bytes accessed | tf_op | source)
XLA Modules:
  0.0 1201.9 jit_solution(3492719368294546650)
XLA Ops:
  9.7 34.3 %gather_fusion = s32[6144]{0:T(1024)S(1)} fusion(s32[2048]{0:T(1024)S(1)} %bitcast.160, s32[6144]{0:T(1024)S(1)} %broadcast_clamp_fusion.1), kind=kCustom, calls=%fused_computation.clone | custom fusion | bytes 73728 | tf_op jit(solution)/shard_map/jit(_take)/gather | solution.py:98
  44.6 23.0 %scatter_custom_fusion = s32[6144]{0:T(1024)S(1)} fusion(s32[6144]{0:T(1024)S(1)} %reshape.282, s32[6144]{0:T(1024)S(1)} %reshape.284, s32[]{:T(128)} %constant.20.clone.1), kind=kCustom, calls=%fused_computation.120 | custom fusion | bytes 24580
  67.9 34.3 %gather_fusion.1 = s32[6144]{0:T(1024)S(1)} fusion(s32[2048]{0:T(1024)S(1)} %convert_reduce_fusion.4, s32[6144]{0:T(1024)S(1)} %broadcast_clamp_fusion), kind=kCustom, calls=%fused_computation.2.clone | custom fusion | bytes 73728 | tf_op jit(solution)/shard_map/jit(_take)/gather | solution.py:102
  148.3 32.3 %gather_fusion.4 = bf16[6144,64]{1,0:T(8,128)(2,1)S(1)} fusion(bf16[3,2048,64]{2,1,0:T(8,128)(2,1)S(1)} %bitcast.163, s32[6144]{0:T(1024)S(1)} %reshape.300), kind=kCustom, calls=%fused_computation.4.clone | custom fusion | bytes 1622016 | tf_op jit(solution)/shard_map/jit(take_along_axis)/gather | solution.py:40
  186.0 32.3 %gather_fusion.3 = bf16[6144,64]{1,0:T(8,128)(2,1)S(1)} fusion(bf16[3,2048,64]{2,1,0:T(8,128)(2,1)S(1)} %bitcast.164, s32[6144]{0:T(1024)S(1)} %reshape.300), kind=kCustom, calls=%fused_computation.3.clone | custom fusion | bytes 1622016 | tf_op jit(solution)/shard_map/jit(take_along_axis)/gather | solution.py:40
  223.7 32.3 %gather_fusion.2 = bf16[6144,64]{1,0:T(8,128)(2,1)S(1)} fusion(bf16[3,2048,64]{2,1,0:T(8,128)(2,1)S(1)} %bitcast.165, s32[6144]{0:T(1024)S(1)} %reshape.300), kind=kCustom, calls=%fused_computation.1.clone | custom fusion | bytes 1622016 | tf_op jit(solution)/shard_map/jit(take_along_axis)/gather | solution.py:40
  264.6 32.3 %gather_fusion.5 = bf16[6144,64]{1,0:T(8,128)(2,1)S(1)} fusion(bf16[3,2048,64]{2,1,0:T(8,128)(2,1)S(1)} %bitcast.166, s32[6144]{0:T(1024)S(1)} %reshape.312), kind=kCustom, calls=%fused_computation.5.clone | custom fusion | bytes 1622016 | tf_op jit(solution)/shard_map/jit(take_along_axis)/gather | solution.py:47
  302.2 59.9 %reduce-scatter.19.cloned.1.call-done = bf16[512,768]{1,0:T(8,128)(2,1)} async-done(((bf16[2048,768]{1,0:T(8,128)(2,1)}), bf16[512,768]{1,0:T(8,128)(2,1)}) %reduce-scatter.19.cloned.1.call-update) | async-done | bytes 786448 | tf_op jit(solution)/shard_map/reduce_scatter | solution.py:120
  367.3 62.8 %all-gather.9.cloned.1.call-done = bf16[2048,768]{1,0:T(8,128)(2,1)} async-done(((bf16[512,768]{1,0:T(8,128)(2,1)}), bf16[2048,768]{1,0:T(8,128)(2,1)}) %all-gather.9.cloned.1.call-update) | async-done | bytes 3145744 | tf_op jit(solution)/shard_map/all_gather | solution.py:126
  461.0 60.3 %reduce-scatter.21.cloned.1.call-done = bf16[512,768]{1,0:T(8,128)(2,1)} async-done(((bf16[2048,768]{1,0:T(8,128)(2,1)}), bf16[512,768]{1,0:T(8,128)(2,1)}) %reduce-scatter.21.cloned.1.call-update) | async-done | bytes 786448 | tf_op jit(solution)/shard_map/reduce_scatter | solution.py:129
  528.3 63.3 %all-gather.15.cloned.1.call-done = bf16[2048,768]{1,0:T(8,128)(2,1)} async-done(((bf16[512,768]{1,0:T(8,128)(2,1)}), bf16[2048,768]{1,0:T(8,128)(2,1)}) %all-gather.15.cloned.1.call-update) | async-done | bytes 3145744 | tf_op jit(solution)/shard_map/all_gather | solution.py:138
  606.2 59.0 %reduce-scatter.23.cloned.1.call-done = bf16[512,768]{1,0:T(8,128)(2,1)} async-done(((bf16[2048,768]{1,0:T(8,128)(2,1)}), bf16[512,768]{1,0:T(8,128)(2,1)}) %reduce-scatter.23.cloned.1.call-update) | async-done | bytes 786448 | tf_op jit(solution)/shard_map/reduce_scatter | solution.py:142
  671.2 63.1 %all-gather.17.cloned.1.call-done = bf16[2048,768]{1,0:T(8,128)(2,1)} async-done(((bf16[512,768]{1,0:T(8,128)(2,1)}), bf16[2048,768]{1,0:T(8,128)(2,1)}) %all-gather.17.cloned.1.call-update) | async-done | bytes 3145744 | tf_op jit(solution)/shard_map/all_gather | solution.py:154
  738.2 60.6 %gather_fusion.6 = bf16[6144,64]{1,0:T(8,128)(2,1)} fusion(bf16[3,2048,64]{2,1,0:T(8,128)(2,1)S(1)} %bitcast.161, s32[6144]{0:T(1024)S(1)} %reshape.300), kind=kCustom, calls=%fused_computation.6.clone | custom fusion | bytes 1622016 | tf_op jit(solution)/shard_map/jit(take_along_axis)/gather | solution.py:40
  814.8 32.3 %gather_fusion.9 = bf16[6144,64]{1,0:T(8,128)(2,1)S(1)} fusion(bf16[3,2048,64]{2,1,0:T(8,128)(2,1)S(1)} %bitcast.167, s32[6144]{0:T(1024)S(1)} %reshape.312), kind=kCustom, calls=%fused_computation.9.clone | custom fusion | bytes 1622016 | tf_op jit(solution)/shard_map/jit(take_along_axis)/gather | solution.py:47
  850.3 32.3 %gather_fusion.7 = bf16[6144,64]{1,0:T(8,128)(2,1)S(1)} fusion(bf16[3,2048,64]{2,1,0:T(8,128)(2,1)S(1)} %bitcast.168, s32[6144]{0:T(1024)S(1)} %reshape.312), kind=kCustom, calls=%fused_computation.7.clone | custom fusion | bytes 1622016 | tf_op jit(solution)/shard_map/jit(take_along_axis)/gather | solution.py:47
  885.8 32.3 %gather_fusion.8 = bf16[6144,64]{1,0:T(8,128)(2,1)S(1)} fusion(bf16[3,2048,64]{2,1,0:T(8,128)(2,1)S(1)} %bitcast.162, s32[6144]{0:T(1024)S(1)} %reshape.312), kind=kCustom, calls=%fused_computation.8.clone | custom fusion | bytes 1622016 | tf_op jit(solution)/shard_map/jit(take_along_axis)/gather | solution.py:47
  957.0 19.2 %all-reduce.1 = (f32[768]{0:T(1024)S(1)}, f32[768]{0:T(1024)S(1)}, f32[768]{0:T(1024)S(1)}, f32[768]{0:T(1024)S(1)}, f32[768]{0:T(1024)S(1)}, /*index=5*/f32[307...) all-reduce(f32[768]{0:T(1024)S(1)} %dynamic_update_slice.9, ...), channel_id=1, replica_groups=mesh['dp'=8,'tensor'=4] {'tensor'}, use_global_device_ids=true, to_apply=%region_20.23 | all-reduce | flops 9216 | bytes 73728 | tf_op jit(solution)/shard_map/psum | solution.py:212
  976.2 23.7 %all-reduce = (f32[768]{0:T(1024)S(1)}, f32[768]{0:T(1024)S(1)}, f32[768]{0:T(1024)}, f32[768]{0:T(1024)}, f32[768]{0:T(1024)}, /*index=5*/f32[3072]{0:T(1024)S(1)}, f32[768]{0:T(1024)}, f32[768]{0:T(1024)}, f32[768]{0:T(1024)}) all-reduce(f32[768]{0:T(1024)S(1)} %get-tuple-element.103, ...), channel_id=1, replica_groups=mesh['dp'=8,'tensor'=4] {'dp'}, use_global_device_ids=true, to_apply=%region_21.24 | all-reduce | flops 9216 | bytes 73728 | tf_op jit(solution)/shard_map/psum | solution.py:211
  1006.0 26.1 %reduce-scatter.27.cloned.1.call-done = f32[96,768]{1,0:T(8,128)} async-done(((f32[768,768]{1,0:T(8,128)}), f32[96,768]{1,0:T(8,128)}) %reduce-scatter.27.cloned.1.call-update) | async-done | bytes 294928 | tf_op jit(solution)/shard_map/reduce_scatter | solution.py:249
  1032.1 46.5 %reduce-scatter.29.cloned.1.call-done = f32[768,96]{0,1:T(8,128)} async-done(((f32[768,768]{0,1:T(8,128)}), f32[768,96]{0,1:T(8,128)}) %reduce-scatter.29.cloned.1.call-update) | async-done | bytes 294928 | tf_op jit(solution)/shard_map/reduce_scatter | solution.py:250
  1078.6 38.7 %reduce-scatter.35.cloned.1.call-done = f32[96,192]{1,0:T(8,128)} async-done(((f32[768,192]{1,0:T(8,128)}), f32[96,192]{1,0:T(8,128)}) %reduce-scatter.35.cloned.1.call-update) | async-done | bytes 73744
  1117.3 38.6 %reduce-scatter.31.cloned.1.call-done = f32[96,192]{1,0:T(8,128)} async-done(((f32[768,192]{1,0:T(8,128)}), f32[96,192]{1,0:T(8,128)}) %reduce-scatter.31.cloned.1.call-update) | async-done | bytes 73744
  1155.9 38.7 %reduce-scatter.33.cloned.1.call-done = f32[96,192]{1,0:T(8,128)} async-done(((f32[768,192]{1,0:T(8,128)}), f32[96,192]{1,0:T(8,128)}) %reduce-scatter.33.cloned.1.call-update) | async-done | bytes 73744
  (257 shorter events, 207.4 us)
Async XLA Ops:
  8.0 136.3 %all-gather.7.cloned.1.call-start = ((), (), s32[]{:S(2)}) async-start(), calls=%async_computation.10 | async-start | bytes 3932160 | tf_op jit(solution)/shard_map/all_gather | solution.py:105
  8.8 353.3 %reduce-scatter.19.cloned.1.call-start = ((), (), s32[]{:S(2)}) async-start(), calls=%async_computation.11 | async-start | bytes 3932160 | tf_op jit(solution)/shard_map/reduce_scatter | solution.py:120
  67.9 66.7 %copy-start.38 = (bf16[96,192]{1,0:T(8,128)(2,1)S(1)}, bf16[96,192]{1,0:T(8,128)(2,1)}, u32[]{:S(2)}) copy-start(bf16[96,192]{1,0:T(8,128)(2,1)} %param.32) | copy-start | bytes 110596
  67.9 76.4 %copy-start.49 = (f32[192]{0:T(256)S(1)}, f32[192]{0:T(256)}, u32[]{:S(2)}) copy-start(f32[192]{0:T(256)} %param.33) | copy-start | bytes 2308
  298.6 63.5 %copy-start.33 = (f32[768]{0:T(1024)S(1)}, f32[768]{0:T(1024)}, u32[]{:S(2)}) copy-start(f32[768]{0:T(1024)} %param.35) | copy-start | bytes 9220
  301.3 63.9 %copy-start.35 = (f32[768]{0:T(1024)S(1)}, f32[768]{0:T(1024)}, u32[]{:S(2)}) copy-start(f32[768]{0:T(1024)} %param.36) | copy-start | bytes 9220
  301.3 63.9 %copy-start.41 = (f32[768]{0:T(1024)S(1)}, f32[768]{0:T(1024)}, u32[]{:S(2)}) copy-start(f32[768]{0:T(1024)} %param.37) | copy-start | bytes 9220
  301.4 65.9 %all-gather.11.cloned.1.call-start = ((), (), s32[]{:S(2)}) async-start(), calls=%async_computation.13 | async-start | bytes 1327104 | tf_op jit(solution)/shard_map/all_gather | solution.py:92
  301.9 128.1 %copy-start.48 = (f32[768]{0:T(1024)S(1)}, f32[768]{0:T(1024)}, u32[]{:S(2)}) copy-start(f32[768]{0:T(1024)} %param.39) | copy-start | bytes 9220
  301.9 128.1 %all-gather.9.cloned.1.call-start = ((), (), s32[]{:S(2)}) async-start(), calls=%async_computation.12 | async-start | bytes 3932160 | tf_op jit(solution)/shard_map/all_gather | solution.py:126
  366.6 87.8 %all-gather.13.cloned.1.call-start = ((), (), s32[]{:S(2)}) async-start(), calls=%async_computation.14 | async-start | bytes 1327104 | tf_op jit(solution)/shard_map/all_gather | solution.py:93
  367.2 154.1 %reduce-scatter.21.cloned.1.call-start = ((), (), s32[]{:S(2)}) async-start(), calls=%async_computation.15 | async-start | bytes 3932160 | tf_op jit(solution)/shard_map/reduce_scatter | solution.py:129
  461.0 130.6 %all-gather.15.cloned.1.call-start = ((), (), s32[]{:S(2)}) async-start(), calls=%async_computation.16 | async-start | bytes 3932160 | tf_op jit(solution)/shard_map/all_gather | solution.py:138
  528.0 137.1 %reduce-scatter.23.cloned.1.call-start = ((), (), s32[]{:S(2)}) async-start(), calls=%async_computation.17 | async-start | bytes 3932160 | tf_op jit(solution)/shard_map/reduce_scatter | solution.py:142
  606.1 128.2 %all-gather.17.cloned.1.call-start = ((), (), s32[]{:S(2)}) async-start(), calls=%async_computation.18 | async-start | bytes 3932160 | tf_op jit(solution)/shard_map/all_gather | solution.py:154
  668.4 65.9 %copy-start.17 = (bf16[192,768]{0,1:T(8,128)(2,1)S(1)}, bf16[192,768]{0,1:T(8,128)(2,1)}, u32[]{:S(2)}) copy-start(bf16[192,768]{0,1:T(8,128)(2,1)} %all_gather.34) | copy-start | bytes 884740
  670.7 331.1 %reduce-scatter.37.cloned.1.call-start = ((), (), s32[]{:S(2)}) async-start(), calls=%async_computation.25 | async-start | bytes 884736
  813.7 189.8 %reduce-scatter.25.cloned.1.call-start = ((), (), s32[]{:S(2)}) async-start(), calls=%async_computation.19 | async-start | bytes 3932160 | tf_op jit(solution)/shard_map/reduce_scatter | solution.py:184
  925.5 106.7 %reduce-scatter.27.cloned.1.call-start = ((), (), s32[]{:S(2)}) async-start(), calls=%async_computation.20 | async-start | bytes 2654208 | tf_op jit(solution)/shard_map/reduce_scatter | solution.py:249
  933.4 145.2 %reduce-scatter.29.cloned.1.call-start = ((), (), s32[]{:S(2)}) async-start(), calls=%async_computation.21 | async-start | bytes 2654208 | tf_op jit(solution)/shard_map/reduce_scatter | solution.py:250
  940.7 176.6 %reduce-scatter.35.cloned.1.call-start = ((), (), s32[]{:S(2)}) async-start(), calls=%async_computation.24 | async-start | bytes 884736
  945.8 210.1 %reduce-scatter.31.cloned.1.call-start = ((), (), s32[]{:S(2)}) async-start(), calls=%async_computation.22 | async-start | bytes 884736
  950.9 243.7 %reduce-scatter.33.cloned.1.call-start = ((), (), s32[]{:S(2)}) async-start(), calls=%async_computation.23 | async-start | bytes 884736
  951.0 243.6 %copy-start.1 = (s32[1,2048]{1,0:T(1,128)S(1)}, s32[1,2048]{1,0:T(1,128)}, u32[]{:S(2)}) copy-start(s32[1,2048]{1,0:T(1,128)} %param.27) | copy-start | bytes 24580
  (45 other events, 759.2 us)
Sparse Core Ops, SparseCore 0:
  10.4 66.1 all-gather.6
  301.5 60.5 reduce-scatter.18
  528.2 63.4 all-gather.14
  670.9 63.4 all-gather.16
Sparse Core Ops, SparseCore 1:
  303.7 24.1 all-gather.10
  366.7 63.3 all-gather.8
  431.8 22.5 all-gather.12
  461.0 60.2 reduce-scatter.20
  606.2 58.9 reduce-scatter.22
  813.8 33.6 reduce-scatter.36
  925.5 60.4 reduce-scatter.24
  989.8 42.3 reduce-scatter.26
  1036.3 42.3 reduce-scatter.28
  1082.4 34.9 reduce-scatter.34
  1120.9 34.9 reduce-scatter.30
  1159.6 34.9 reduce-scatter.32
